TPU v7x, 512 devices: a whole 4x8x8 slice. The times are simulated.
512 devices in a mesh: cls: 64 (over x, z, y_hi), dp: 8 (over y_lo, core).
Axes of the slice: x: 4, y: 8 (y_hi: 2, y_lo: 4; y = y_hi * 4 + y_lo), z: 8, core: 2. Of those that a mesh axis runs over, the one named last changes fastest.
Arguments:
- features: bfloat16 [65536, 512], P(('cls', 'dp')), may hold values from -6 to 6
- labels: int32 [65536], P(('cls', 'dp')), may hold values from 0 to 16383, as said below
- weights: float32 [65536, 512], P('cls'), may hold values from -0.25 to 0.25
- sampled: int32 [16384], P('cls'), may hold values from 0 to 1023, as said below
Outputs:
- sample_loss: float32 [65536], P(('cls', 'dp'))
- weight_grad: float32 [16384, 512], P(('cls', 'dp'))
Inputs may be any that keep to these rules, and one draw needn't show every extreme that they name: The owner of a label is label // 256. In the rows of one device (aligned blocks of 128 rows) exactly one owner receives 4 of the labels and every other owner fewer. `sampled`: each aligned block of 256 entries holds distinct rows of the owner's bank.
All inputs are finite; a program needn't handle non-finite values.
Results may differ from a plain program's by a relative error of at most 0.0038.
Values may be sent and summed in bfloat16 or wider, within the bound.
A program may use at most 64 MiB of HBM per device.

v0:
```python
import math
import jax
import jax.numpy as jnp
from jax import lax
from jax.sharding import PartitionSpec as P

logit_scale = 64.0
margin = 0.35
epsilon = 1e-06


def normalize_rows(matrix):
    squares = jnp.sum(matrix * matrix, axis=1, keepdims=True)
    return lax.rsqrt(squares + epsilon)


def logits_of(feat_block, label_block, class_block, class_ids):
    cosine = jnp.dot(feat_block, class_block.T, preferred_element_type=jnp.float32)
    target_hit = label_block[:, None] == class_ids[None, :]
    logits = logit_scale * (cosine - margin * target_hit.astype(jnp.float32))
    return (logits, target_hit)


def per_device(features, labels, weights, sampled):
    groups = lax.axis_size("cls")
    replicas = lax.axis_size("dp")
    position = lax.axis_index("cls")
    local_rows = features.shape[0]
    feature_width = features.shape[1]
    classes = sampled.shape[0]
    capacity = local_rows // groups + 2
    feat_wide = features.astype(jnp.float32)
    unit_feats = (feat_wide * normalize_rows(feat_wide)).astype(jnp.bfloat16)
    chosen = weights[sampled]
    inverse_norm = normalize_rows(chosen)
    unit_f32 = chosen * inverse_norm
    unit_rows = unit_f32.astype(jnp.bfloat16)
    owner_ids = labels // classes
    column = labels % classes
    owner_hits = (owner_ids[:, None] == jnp.arange(groups, dtype=jnp.int32)[None, :]).astype(
        jnp.int32
    )
    earlier = jnp.cumsum(owner_hits, axis=0) - owner_hits
    ranking = jnp.sum(earlier * owner_hits, axis=1)
    buffer_slot = owner_ids * capacity + ranking
    slot_codes = jnp.arange(local_rows, dtype=jnp.int32) * classes + column
    outgoing = jnp.full((groups * capacity,), -1, jnp.int32).at[buffer_slot].set(slot_codes)
    outgoing = outgoing.reshape(groups, capacity)
    gathered = lax.all_gather(unit_feats, "cls", axis=0, tiled=True)
    group_rows = gathered.shape[0]

    def decode(incoming):
        is_valid = incoming >= 0
        safe_code = jnp.maximum(incoming, 0)
        source_row = (
            jnp.arange(incoming.shape[0], dtype=jnp.int32)[:, None] * local_rows
            + safe_code // classes
        )
        return (is_valid, source_row, safe_code % classes)

    incoming = lax.all_to_all(outgoing, "cls", split_axis=0, concat_axis=0, tiled=True)
    is_valid, source_row, class_col = decode(incoming)
    feat_rows = gathered[source_row].astype(jnp.float32)
    class_rows = unit_rows[class_col].astype(jnp.float32)
    cosine = jnp.sum(feat_rows * class_rows, axis=2)
    values = logit_scale * (cosine - margin)
    replies = lax.all_to_all(values, "cls", split_axis=0, concat_axis=0, tiled=True)
    replies, incoming = (replies, incoming)
    is_valid, source_row, class_col = decode(incoming)
    drop_index = jnp.where(is_valid, source_row, group_rows).reshape(-1)
    label_local = (
        jnp.full((group_rows,), -1, jnp.int32)
        .at[drop_index]
        .set(class_col.reshape(-1), mode="drop")
    )
    block_rows = math.gcd(group_rows, 512)
    count_blocks = group_rows // block_rows
    feat_blocks = gathered.reshape(count_blocks, block_rows, feature_width)
    label_blocks = label_local.reshape(count_blocks, block_rows)
    all_ids = jnp.arange(classes, dtype=jnp.int32)

    def first_pass(operands):
        logits, target_hit = logits_of(operands[0], operands[1], unit_rows, all_ids)
        part_sum = jnp.sum(jnp.exp(logits - logit_scale), axis=1)
        part_target = jnp.sum(jnp.where(target_hit, logits, 0.0), axis=1)
        return (part_sum, part_target)

    part_sum, part_target = lax.map(first_pass, (feat_blocks, label_blocks))
    part_sum = part_sum.reshape(group_rows)
    part_target = part_target.reshape(group_rows)
    own_start = position * local_rows
    totals = lax.psum(part_sum, "cls")
    own_target = replies.reshape(-1)[buffer_slot]
    own_total = lax.dynamic_slice_in_dim(totals, own_start, local_rows)
    sample_loss = logit_scale + jnp.log(own_total) - own_target
    total_blocks = totals.reshape(count_blocks, block_rows)
    class_ids = jnp.arange(lax.axis_size("dp") * (classes // replicas), dtype=jnp.int32)

    def accumulate(running, triple):
        logits, target_hit = logits_of(triple[0], triple[1], unit_rows, class_ids)
        softmax = jnp.exp(logits - logit_scale) / triple[2][:, None]
        grads_low = (logit_scale * (softmax - target_hit.astype(jnp.float32)) / replicas).astype(
            jnp.bfloat16
        )
        return (running + jnp.dot(grads_low.T, triple[0], preferred_element_type=jnp.float32), None)

    start_grad = jnp.zeros(
        (lax.axis_size("dp") * (classes // replicas), feature_width), jnp.float32
    )
    unit_grad, _ = lax.scan(accumulate, start_grad, (feat_blocks, label_blocks, total_blocks))
    radial = jnp.sum(unit_f32 * unit_grad, axis=1, keepdims=True)
    weight_grad = lax.psum_scatter(
        inverse_norm * (unit_grad - unit_f32 * radial), "dp", scatter_dimension=0, tiled=True
    )
    return (sample_loss, weight_grad)


def solution(mesh):
    in_specs = (P(("cls", "dp"), None), P(("cls", "dp")), P("cls", None), P("cls"))
    out_specs = (P(("cls", "dp")), P(("cls", "dp"), None))
    return jax.shard_map(
        per_device, mesh=mesh, in_specs=in_specs, out_specs=out_specs, check_vma=False
    )
```

profile of v0, /device:TPU:16, one launch (start us, length us, event | category | flops | bytes accessed | tf_op | source)
XLA Modules:
  0.0 773.6 jit_solution(14654492984104845493)
XLA Ops:
  12.9 17.2 %all-to-all-start = ((s32[64,1,4]{2,1,0:T(1,128)}), s32[64,1,4]{2,1,0:T(1,128)S(1)}, u32[]{:S(2)}, u32[]{:S(2)}) async-start(s32[64,1,4]{2,1,0:T(1,128)} %bitcast.1), calls=%async_computation | async-start | bytes 65536 | tf_op jit(solution)/shard_map/all_to_all | solution.py:61
  32.8 11.6 %all-to-all-done = s32[64,1,4]{2,1,0:T(1,128)S(1)} async-done(((s32[64,1,4]{2,1,0:T(1,128)}), s32[64,1,4]{2,1,0:T(1,128)S(1)}, u32[]{:S(2)}, u32[]{:S(2)}) %all-to-all-start) | async-done | bytes 1056 | tf_op jit(solution)/shard_map/all_to_all | solution.py:61
  46.6 159.0 %all-gather.2.cloned.1.call-done = bf16[8192,512]{1,0:T(8,128)(2,1)} async-done(((bf16[128,512]{1,0:T(8,128)(2,1)}), bf16[8192,512]{1,0:T(8,128)(2,1)}) %all-gather.2.cloned.1.call-update) | async-done | bytes 8388624 | tf_op jit(solution)/shard_map/all_gather | solution.py:49
  205.6 44.7 %while.26 = (s32[]{:T(128)}, f32[16,512]{1,0:T(8,128)}, bf16[16,512,512]{2,1,0:T(8,128)(2,1)}, bf16[256,512]{1,0:T(8,128)(2,1)S(1)}, s32[16,512]{1,0:T(8,128)S(1)}, /*index=5*/s32[]{:T(128)}, s32[]{:T(128)}) while((s32[]{:T(128)}, f32[16,512]{1,0:T(8,128)}, bf16[16,512,512]{2,1,0:T(8,128)(2,1)}, bf16[256,512]{1,0:T(8,128)(2,1)S(1)}, ...), condition=%wide.region_8.9_spmd.clone, body=%wide.region_6.8_spmd.clone.sunk | while | flops 135003648 | bytes 798817 | solution.py:88
  251.1 435.4 %psum.7 = f32[8192]{0:T(1024)S(1)} all-reduce(f32[8192]{0:T(1024)S(1)} %bitcast.77), channel_id=1, replica_groups=mesh['cls'=64,'dp'=8] {'cls'}, use_global_device_ids=true, to_apply=%region_9.10 | all-reduce | flops 8192 | bytes 65536 | tf_op jit(solution)/shard_map/psum | solution.py:92
  686.5 47.0 %while.27 = (s32[]{:T(128)}, f32[256,512]{1,0:T(8,128)S(1)}, bf16[16,512,512]{2,1,0:T(8,128)(2,1)}, bf16[256,512]{1,0:T(8,128)(2,1)S(1)}, s32[16,512]{1,0:T(8,12...) while((s32[]{:T(128)}, f32[256,512]{1,0:T(8,128)S(1)}, bf16[16,512,512]{2,1,0:T(8,128)(2,1)}, ...), condition=%wide.region_12.13_spmd.clone, body=%wide.region_11.12_spmd.clone.sunk | while | flops 270008320 | bytes 2373230 | solution.py:110
  687.2 2.1 convolution_add_fusion.2
  690.1 2.1 convolution_add_fusion.2
  693.1 2.1 convolution_add_fusion.2
  696.0 2.2 convolution_add_fusion.2
  698.9 2.1 convolution_add_fusion.2
  701.9 2.2 convolution_add_fusion.2
  704.8 2.1 convolution_add_fusion.2
  707.7 2.1 convolution_add_fusion.2
  713.6 2.2 convolution_add_fusion.2
  716.5 2.1 convolution_add_fusion.2
  719.4 2.2 convolution_add_fusion.2
  722.4 2.2 convolution_add_fusion.2
  725.3 2.3 convolution_add_fusion.2
  728.4 2.2 convolution_add_fusion.2
  731.3 2.1 convolution_add_fusion.2
  738.1 5.7 gather_fusion.1
  744.7 4.6 all-to-all-start.1
  749.4 14.2 %all-to-all-done.1 = f32[64,1,4]{2,1,0:T(1,128)S(1)} async-done(((f32[64,1,4]{2,1,0:T(1,128)}), f32[64,1,4]{2,1,0:T(1,128)S(1)}, u32[]{:S(2)}, u32[]{:S(2)}) %all-to-all-start.1) | async-done | bytes 1056 | tf_op jit(solution)/shard_map/all_to_all | solution.py:67
  (152 shorter events, 78.4 us)
Async XLA Ops:
  7.2 23.7 %copy-start = (f32[1024,512]{1,0:T(8,128)S(1)}, f32[1024,512]{1,0:T(8,128)}, u32[]{:S(2)}) copy-start(f32[1024,512]{1,0:T(8,128)} %param.10) | copy-start | bytes 6291460
  7.2 198.4 %all-gather.2.cloned.1.call-start = ((), (), s32[]{:S(2)}) async-start(), calls=%async_computation.3 | async-start | bytes 8519680 | tf_op jit(solution)/shard_map/all_gather | solution.py:49
  11.2 19.0 %copy-start.4 = (s32[128]{0:T(128)}, s32[128]{0:T(128)S(1)}, u32[]{:S(2)}) copy-start(s32[128]{0:T(128)S(1)} %compare_select_fusion.4) | copy-start | bytes 1540
  12.9 31.5 %all-to-all-start = ((s32[64,1,4]{2,1,0:T(1,128)}), s32[64,1,4]{2,1,0:T(1,128)S(1)}, u32[]{:S(2)}, u32[]{:S(2)}) async-start(s32[64,1,4]{2,1,0:T(1,128)} %bitcast.1), calls=%async_computation | async-start | bytes 65536 | tf_op jit(solution)/shard_map/all_to_all | solution.py:61
  30.2 736.6 %reduce-scatter.2.cloned.1.call-start = ((), (), s32[]{:S(2)}) async-start(), calls=%async_computation.4 | async-start | bytes 589824 | tf_op jit(solution)/shard_map/reduce_scatter | solution.py:112
  32.0 0.6 copy-start.2
  32.1 12.4 %copy-start.3 = (s32[64]{0:T(128)}, s32[64]{0:T(128)S(1)}, u32[]{:S(2)}) copy-start(s32[64]{0:T(128)S(1)} %iota_multiply_fusion) | copy-start | bytes 772
  250.3 0.8 copy-start.1
  733.5 15.9 %copy-start.5 = (s32[128]{0:T(128)S(1)}, s32[128]{0:T(128)}, u32[]{:S(2)}) copy-start(s32[128]{0:T(128)} %copy-done.4) | copy-start | bytes 1540
  744.7 18.9 %all-to-all-start.1 = ((f32[64,1,4]{2,1,0:T(1,128)}), f32[64,1,4]{2,1,0:T(1,128)S(1)}, u32[]{:S(2)}, u32[]{:S(2)}) async-start(f32[64,1,4]{2,1,0:T(1,128)} %bitcast.10), calls=%async_computation.1 | async-start | bytes 65536 | tf_op jit(solution)/shard_map/all_to_all | solution.py:67
Sparse Core Ops, SparseCore 0:
  12.5 193.0 all-gather.1
  736.2 23.3 reduce-scatter.1
where the time goes:
time: 777 us; the launch traced here: 774 us
  blocking collectives  435 us (56%)
  waiting for transfers between devices  185 us (24%)
  matrix products  57.7 us (7%)
  local copies, waits for them, and re-layouts  49.1 us (6%)
  starting transfers between devices  21.9 us (3%)
  between operations  14.4 us (2%)
  other arithmetic  9.74 us (1%)
    psum x1, blocking collectives, per_device(): totals = lax.psum(part_sum, 'cls')  435 us
    all_gather x1, waiting for transfers between devices, per_device(): gathered = lax.all_gather(unit_feats, 'cls', axis=0, tiled=True)  159 us
    dot_general x16, matrix products, accumulate(): jnp.dot(grads_low.T, triple[0], preferred_element_type=jnp.float32)  34.6 us
    dot_general x16, matrix products, logits_of(): jnp.dot(feat_block, class_block.T, preferred_element_type=jnp.float32)  23 us
    dynamic_update_slice x16, local copies, waits for them, and re-layouts, per_device(): part_sum, part_target = lax.map(first_pass, (feat_blocks, label_blocks))  21.5 us
    all_to_all x1, starting transfers between devices, per_device(): lax.all_to_all(outgoing, 'cls', split_axis=0, concat_axis=0, tiled=True)  17.2 us
  transfers between devices with their start and end apart: 4, of which 3 were waited for; matrix products, arithmetic and copies ran while one was open for 2% of the time, Pallas kernels for 0%

commit v1 on v0

--- a/solution.py
+++ b/solution.py
@@ -46,7 +46,15 @@
     slot_codes = jnp.arange(local_rows, dtype=jnp.int32) * classes + column
     outgoing = jnp.full((groups * capacity,), -1, jnp.int32).at[buffer_slot].set(slot_codes)
     outgoing = outgoing.reshape(groups, capacity)
-    gathered = lax.all_gather(unit_feats, "cls", axis=0, tiled=True)
+    gathered = jnp.concatenate(
+        jax.lax.all_to_all(
+            jnp.stack([unit_feats for _ in range(jax.lax.axis_size("cls"))]),
+            axis_name="cls",
+            split_axis=0,
+            concat_axis=0,
+        ),
+        0,
+    )
     group_rows = gathered.shape[0]
 
     def decode(incoming):

time: 777 us -> 846 us (1.089)
  the two profiles are of different devices: /device:TPU:16 before, /device:TPU:8 now
where the time goes in v1:
time: 846 us; the launch traced here: 842 us
  blocking collectives  429 us (51%)
  waiting for transfers between devices  249 us (29%)
  matrix products  57.7 us (7%)
  local copies, waits for them, and re-layouts  53.9 us (6%)
  starting transfers between devices  28.7 us (3%)
  between operations  14.4 us (2%)
    psum x1, blocking collectives, per_device(): totals = lax.psum(part_sum, 'cls')  429 us
    all_to_all x1, waiting for transfers between devices, per_device(): jax.lax.all_to_all(jnp.stack([unit_feats for _ in range(jax.lax.axis_size...  223 us
    dot_general x16, matrix products, accumulate(): jnp.dot(grads_low.T, triple[0], preferred_element_type=jnp.float32)  34.6 us
    dot_general x16, matrix products, logits_of(): jnp.dot(feat_block, class_block.T, preferred_element_type=jnp.float32)  23 us
    dynamic_update_slice x16, local copies, waits for them, and re-layouts, per_device(): part_sum, part_target = lax.map(first_pass, (feat_blocks, label_blocks))  21.5 us
    all_to_all x1, starting transfers between devices, per_device(): lax.all_to_all(outgoing, 'cls', split_axis=0, concat_axis=0, tiled=True)  18.1 us
  transfers between devices with their start and end apart: 4, of which 3 were waited for; matrix products, arithmetic and copies ran while one was open for 2% of the time, Pallas kernels for 0%

profile of v1, /device:TPU:8, one launch (start us, length us, event | category | flops | bytes accessed | tf_op | source)
XLA Modules:
  0.0 842.3 jit_solution(18249755262208067773)
XLA Ops:
  10.2 18.1 %all-to-all-start.1 = ((s32[64,1,4]{2,1,0:T(1,128)}), s32[64,1,4]{2,1,0:T(1,128)S(1)}, u32[]{:S(2)}, u32[]{:S(2)}) async-start(s32[64,1,4]{2,1,0:T(1,128)} %bitcast.1), calls=%async_computation.1 | async-start | bytes 65536 | tf_op jit(solution)/shard_map/all_to_all | solution.py:69
  30.4 12.1 %all-to-all-done.1 = s32[64,1,4]{2,1,0:T(1,128)S(1)} async-done(((s32[64,1,4]{2,1,0:T(1,128)}), s32[64,1,4]{2,1,0:T(1,128)S(1)}, u32[]{:S(2)}, u32[]{:S(2)}) %all-to-all-start.1) | async-done | bytes 1056 | tf_op jit(solution)/shard_map/all_to_all | solution.py:69
  42.5 4.2 stack.2
  46.7 5.9 all-to-all-start
  56.8 222.9 %all-to-all-done = bf16[64,128,512]{2,1,0:T(8,128)(2,1)} async-done(((bf16[64,128,512]{2,1,0:T(8,128)(2,1)}), bf16[64,128,512]{2,1,0:T(8,128)(2,1)}, u32[]{:S(2)}, u32[]{:S(2)}) %all-to-all-start) | async-done | bytes 8388640 | tf_op jit(solution)/shard_map/all_to_all | solution.py:50
  279.7 44.7 %while.26 = (s32[]{:T(128)}, f32[16,512]{1,0:T(8,128)}, bf16[16,512,512]{2,1,0:T(8,128)(2,1)}, bf16[256,512]{1,0:T(8,128)(2,1)S(1)}, s32[16,512]{1,0:T(8,128)S(1)}, /*index=5*/s32[]{:T(128)}, s32[]{:T(128)}) while((s32[]{:T(128)}, f32[16,512]{1,0:T(8,128)}, bf16[16,512,512]{2,1,0:T(8,128)(2,1)}, bf16[256,512]{1,0:T(8,128)(2,1)S(1)}, ...), condition=%wide.region_8.9_spmd.clone, body=%wide.region_6.8_spmd.clone.sunk | while | flops 135003648 | bytes 799317 | solution.py:96
  325.8 429.2 %psum.7 = f32[8192]{0:T(1024)S(1)} all-reduce(f32[8192]{0:T(1024)S(1)} %bitcast.74), channel_id=1, replica_groups=mesh['cls'=64,'dp'=8] {'cls'}, use_global_device_ids=true, to_apply=%region_9.10 | all-reduce | flops 8192 | bytes 65536 | tf_op jit(solution)/shard_map/psum | solution.py:100
  755.0 46.9 %while.27 = (s32[]{:T(128)}, f32[256,512]{1,0:T(8,128)S(1)}, bf16[16,512,512]{2,1,0:T(8,128)(2,1)}, bf16[256,512]{1,0:T(8,128)(2,1)S(1)}, s32[16,512]{1,0:T(8,12...) while((s32[]{:T(128)}, f32[256,512]{1,0:T(8,128)S(1)}, bf16[16,512,512]{2,1,0:T(8,128)(2,1)}, ...), condition=%wide.region_12.13_spmd.clone, body=%wide.region_11.12_spmd.clone.sunk | while | flops 270008320 | bytes 2372711 | solution.py:118
  755.8 2.1 convolution_add_fusion.2
  758.7 2.1 convolution_add_fusion.2
  764.5 2.2 convolution_add_fusion.2
  770.4 2.2 convolution_add_fusion.2
  773.3 2.1 convolution_add_fusion.2
  776.3 2.1 convolution_add_fusion.2
  779.2 2.1 convolution_add_fusion.2
  782.1 2.2 convolution_add_fusion.2
  785.0 2.1 convolution_add_fusion.2
  787.9 2.2 convolution_add_fusion.2
  790.9 2.2 convolution_add_fusion.2
  793.8 2.3 convolution_add_fusion.2
  796.9 2.2 convolution_add_fusion.2
  806.7 5.7 gather_fusion.1
  813.3 4.6 all-to-all-start.2
  817.9 14.3 %all-to-all-done.2 = f32[64,1,4]{2,1,0:T(1,128)S(1)} async-done(((f32[64,1,4]{2,1,0:T(1,128)}), f32[64,1,4]{2,1,0:T(1,128)S(1)}, u32[]{:S(2)}, u32[]{:S(2)}) %all-to-all-start.2) | async-done | bytes 1056 | tf_op jit(solution)/shard_map/all_to_all | solution.py:75
  (154 shorter events, 81.9 us)
Async XLA Ops:
  7.2 45.8 %copy-start = (f32[1024,512]{1,0:T(8,128)S(1)}, f32[1024,512]{1,0:T(8,128)}, u32[]{:S(2)}) copy-start(f32[1024,512]{1,0:T(8,128)} %param.10) | copy-start | bytes 6291460
  8.4 20.9 %copy-start.5 = (s32[128]{0:T(128)}, s32[128]{0:T(128)S(1)}, u32[]{:S(2)}) copy-start(s32[128]{0:T(128)S(1)} %compare_select_fusion.4) | copy-start | bytes 1540
  10.2 32.3 %all-to-all-start.1 = ((s32[64,1,4]{2,1,0:T(1,128)}), s32[64,1,4]{2,1,0:T(1,128)S(1)}, u32[]{:S(2)}, u32[]{:S(2)}) async-start(s32[64,1,4]{2,1,0:T(1,128)} %bitcast.1), calls=%async_computation.1 | async-start | bytes 65536 | tf_op jit(solution)/shard_map/all_to_all | solution.py:69
  46.7 6.2 copy-start.4
  46.7 233.0 %all-to-all-start = ((bf16[64,128,512]{2,1,0:T(8,128)(2,1)}), bf16[64,128,512]{2,1,0:T(8,128)(2,1)}, u32[]{:S(2)}, u32[]{:S(2)}) async-start(bf16[64,128,512]{2,1,0:T(8,128)(2,1)} %stack.2), calls=%async_computation | async-start | bytes 16777216 | tf_op jit(solution)/shard_map/all_to_all | solution.py:50
  52.6 782.8 %reduce-scatter.2.cloned.1.call-start = ((), (), s32[]{:S(2)}) async-start(), calls=%async_computation.4 | async-start | bytes 589824 | tf_op jit(solution)/shard_map/reduce_scatter | solution.py:120
  52.7 1.3 copy-start.3
  54.0 0.6 copy-start.2
  324.4 0.6 copy-start.1
  802.0 15.9 %copy-start.6 = (s32[128]{0:T(128)S(1)}, s32[128]{0:T(128)}, u32[]{:S(2)}) copy-start(s32[128]{0:T(128)} %copy-done.5) | copy-start | bytes 1540
  813.3 18.9 %all-to-all-start.2 = ((f32[64,1,4]{2,1,0:T(1,128)}), f32[64,1,4]{2,1,0:T(1,128)S(1)}, u32[]{:S(2)}, u32[]{:S(2)}) async-start(f32[64,1,4]{2,1,0:T(1,128)} %bitcast.11), calls=%async_computation.2 | async-start | bytes 65536 | tf_op jit(solution)/shard_map/all_to_all | solution.py:75
Sparse Core Ops, SparseCore 0:
  804.7 25.0 reduce-scatter.1
